TPU v7x, 32 devices: a whole 2x2x4 slice. The times are simulated.
32 devices in a mesh: dp: 16 (over z, y, core), mp: 2 (over x).
Axes of the slice: x: 2, y: 2, z: 4, core: 2. Of those that a mesh axis runs over, the one named last changes fastest.
Arguments:
- tokens_in: bfloat16 [4096, 2048], P(('dp', 'mp')), may hold values from -6 to 6
- teacher: bfloat16 [4096, 2048], P(('dp', 'mp')), may hold values from -6 to 6
- valid_mask: int32 [16, 256], P('dp', 'mp'), may hold values from 0 to 1, as said below
- group_of: int32 [16], replicated, may hold values from 0 to 1, as said below
- prompt_len: int32 [2], replicated, may hold values from 128 to 256
- ln1_gain: bfloat16 [2048], P('dp'), may hold values from 0.5 to 1.5
- ln1_bias: bfloat16 [2048], P('dp'), may hold values from -2 to 2
- w_query: bfloat16 [2048, 2048], P('dp', 'mp'), may hold values from -0.125 to 0.125
- w_key: bfloat16 [2048, 2048], P('dp', 'mp'), may hold values from -0.125 to 0.125
- w_value: bfloat16 [2048, 4096], P('dp', 'mp'), may hold values from -0.125 to 0.125
- w_gate: bfloat16 [2048, 4096], P('dp', 'mp'), may hold values from -0.125 to 0.125
- w_out: bfloat16 [2048, 4096], P('dp', 'mp'), may hold values from -0.1875 to 0.1875
- ln2_gain: bfloat16 [2048], P('dp'), may hold values from 0.5 to 1.5
- ln2_bias: bfloat16 [2048], P('dp'), may hold values from -2 to 2
- w_up: bfloat16 [2048, 4096], P('dp', 'mp'), may hold values from -0.125 to 0.125
- w_down: bfloat16 [2048, 4096], P('dp', 'mp'), may hold values from -0.125 to 0.125
Outputs:
- block_out: float32 [4096, 2048], P(('dp', 'mp'))
- grad_tokens: float32 [4096, 2048], P(('dp', 'mp'))
- loss: float32 [], replicated
- grad_ln1_gain: float32 [2048], P('dp')
- grad_ln1_bias: float32 [2048], P('dp')
- grad_w_query: float32 [2048, 2048], P('dp', 'mp')
- grad_w_key: float32 [2048, 2048], P('dp', 'mp')
- grad_w_value: float32 [2048, 4096], P('dp', 'mp')
- grad_w_gate: float32 [2048, 4096], P('dp', 'mp')
- grad_w_out: float32 [2048, 4096], P('dp', 'mp')
- grad_ln2_gain: float32 [2048], P('dp')
- grad_ln2_bias: float32 [2048], P('dp')
- grad_w_up: float32 [2048, 4096], P('dp', 'mp')
- grad_w_down: float32 [2048, 4096], P('dp', 'mp')
Inputs may be any that keep to these rules, and one draw needn't show every extreme that they name: `valid_mask`: in each row the ones form a leading run of one or more positions, zeros follow. `group_of`: each group number is held by exactly 8 segments; a group's prompt is its lowest-numbered segment, the others are its continuations.
All inputs are finite; a program needn't handle non-finite values.
Results may differ from a plain program's by a relative error of at most 0.013.
Values may be sent and summed in bfloat16 or wider, within the bound.
A program may use at most 192 MiB of HBM per device.

v0:
```python
import math
import jax
import jax.numpy as jnp
from jax import lax
from jax.sharding import PartitionSpec as P

DK = 256
DV = 512
EPSILON = 1e-05
GROUP_EPSILON = 0.05


def norm_stats(values, floor_eps):
    center = jnp.mean(values, axis=-1, keepdims=True)
    shifted = values - center
    inv_std = lax.rsqrt(jnp.mean(shifted * shifted, axis=-1, keepdims=True) + floor_eps)
    return (shifted * inv_std, inv_std)


def norm_back(grad_in, normed, inv_std):
    mean_grad = jnp.mean(grad_in, axis=-1, keepdims=True)
    mean_proj = jnp.mean(grad_in * normed, axis=-1, keepdims=True)
    return (grad_in - mean_grad - normed * mean_proj) * inv_std


def xpos_tables(positions, direction):
    half_dim = DK // 2
    pair_index = jnp.arange(half_dim, dtype=jnp.float32)
    frequency = jnp.exp(-(2.0 * pair_index / DK) * math.log(10000.0))
    base_ratio = (2.0 * pair_index / DK + 0.4) / 1.4
    angles = positions[:, None] * frequency[None, :]
    factor = jnp.exp(direction * (positions[:, None] / 512.0) * jnp.log(base_ratio)[None, :])
    return (jnp.cos(angles), jnp.sin(angles), factor)


def rotate_pairs(values, cosine, sine_tab, factor):
    half_dim = values.shape[-1] // 2
    first_half = values[..., :half_dim]
    second = values[..., half_dim:]
    cosine = cosine[:, None, :]
    sine_tab = sine_tab[:, None, :]
    factor = factor[:, None, :]
    return jnp.concatenate(
        [
            (first_half * cosine - second * sine_tab) * factor,
            (second * cosine + first_half * sine_tab) * factor,
        ],
        axis=-1,
    )


def rotate_back(grad_rot, cosine, sine_tab, factor):
    half_dim = grad_rot.shape[-1] // 2
    first_half = grad_rot[..., :half_dim]
    second = grad_rot[..., half_dim:]
    cosine = cosine[:, None, :]
    sine_tab = sine_tab[:, None, :]
    factor = factor[:, None, :]
    return jnp.concatenate(
        [
            (first_half * cosine + second * sine_tab) * factor,
            (second * cosine - first_half * sine_tab) * factor,
        ],
        axis=-1,
    )


def plain_dot(first_op, second_op):
    return jnp.dot(first_op, second_op, preferred_element_type=jnp.float32)


def contract_last(first_op, second_op):
    return lax.dot_general(
        first_op, second_op, (((1,), (1,)), ((), ())), preferred_element_type=jnp.float32
    )


def contract_first(first_op, second_op):
    return lax.dot_general(
        first_op, second_op, (((0,), (0,)), ((), ())), preferred_element_type=jnp.float32
    )


def gather_rows(rows_low):
    return lax.all_gather(rows_low, "mp", axis=0, tiled=True)


def scatter_rows(terms):
    return lax.psum_scatter(terms, "mp", scatter_dimension=0, tiled=True)


def on_device(
    tokens_in,
    teacher,
    valid_mask,
    group_of,
    prompt_len,
    ln1_gain,
    ln1_bias,
    w_query,
    w_key,
    w_value,
    w_gate,
    w_out,
    ln2_gain,
    ln2_bias,
    w_up,
    w_down,
):
    half_rows = tokens_in.shape[0]
    model_dim = tokens_in.shape[1]
    seg_len = half_rows * lax.axis_size("mp")
    seg_count = group_of.shape[0]
    group_count = prompt_len.shape[0]
    heads_local = w_query.shape[1] // DK
    token_total = seg_len * seg_count
    dp_index = lax.axis_index("dp")
    mp_index = lax.axis_index("mp")
    attn_full = (
        lax.all_gather(ln1_gain, "dp", axis=0, tiled=True),
        lax.all_gather(ln1_bias, "dp", axis=0, tiled=True),
        lax.all_gather(w_query, "dp", axis=0, tiled=True),
        lax.all_gather(w_key, "dp", axis=0, tiled=True),
        lax.all_gather(w_value, "dp", axis=0, tiled=True),
        lax.all_gather(w_gate, "dp", axis=0, tiled=True),
        lax.all_gather(w_out, "dp", axis=0, tiled=True),
    )
    ffn_full = (
        lax.all_gather(ln2_gain, "dp", axis=0, tiled=True),
        lax.all_gather(ln2_bias, "dp", axis=0, tiled=True),
        lax.all_gather(w_up, "dp", axis=0, tiled=True),
        lax.all_gather(w_down, "dp", axis=0, tiled=True),
    )
    gain_one = attn_full[0].astype(jnp.float32)
    bias_one = attn_full[1].astype(jnp.float32)
    wq_full, wk_full, wv_full, wg_full, wo_full = (
        attn_full[2],
        attn_full[3],
        attn_full[4],
        attn_full[5],
        attn_full[6],
    )
    gain_two = ffn_full[0].astype(jnp.float32)
    bias_two = ffn_full[1].astype(jnp.float32)
    wu_full, wd_full = (ffn_full[2], ffn_full[3])
    segment_ids = jnp.arange(seg_count, dtype=jnp.int32)
    my_group = jnp.sum(jnp.where(segment_ids == dp_index, group_of, 0))
    first_member = jnp.min(jnp.where(group_of == my_group, segment_ids, seg_count))
    prompt_flag = (first_member == dp_index).astype(jnp.float32)
    group_match = jnp.arange(group_count, dtype=jnp.int32) == my_group
    group_onehot = group_match.astype(jnp.float32)
    prompt_size = jnp.sum(jnp.where(group_match, prompt_len, 0))
    token_ids = jnp.arange(seg_len, dtype=jnp.int32)
    offset = jnp.where(prompt_flag > 0, 0, prompt_size)
    positions = (token_ids + offset).astype(jnp.float32)
    head_ids = (mp_index * heads_local + jnp.arange(heads_local, dtype=jnp.int32)).astype(
        jnp.float32
    )
    log_decay = jnp.log(1.0 - 2.0 ** (-5.0 - head_ids))
    before_end = token_ids < prompt_size
    state_age = (prompt_size - 1 - token_ids).astype(jnp.float32)
    state_weighting = jnp.where(
        (before_end & (prompt_flag > 0))[:, None],
        jnp.exp(log_decay[None, :] * jnp.maximum(state_age, 0.0)[:, None]),
        0.0,
    )
    continuation_factor = (1.0 - prompt_flag) * jnp.exp(
        log_decay[None, :] * (token_ids.astype(jnp.float32) + 1.0)[:, None]
    )
    float_ids = token_ids.astype(jnp.float32)
    distance = float_ids[:, None] - float_ids[None, :]
    decay_mat = jnp.where(
        distance[None] >= 0.0,
        jnp.exp(log_decay[:, None, None] * jnp.maximum(distance, 0.0)[None]),
        0.0,
    )
    own_ids = mp_index * half_rows + jnp.arange(half_rows, dtype=jnp.int32)
    loss_mask = valid_mask[0].astype(jnp.float32) * jnp.where(
        prompt_flag > 0, own_ids < prompt_size, True
    ).astype(jnp.float32)
    token_rows = tokens_in.astype(jnp.float32)
    normed_one, inv_one = norm_stats(token_rows, EPSILON)
    a_all = gather_rows((normed_one * gain_one + bias_one).astype(jnp.bfloat16))
    queries = plain_dot(a_all, wq_full).reshape(seg_len, heads_local, DK)
    keys_raw = plain_dot(a_all, wk_full).reshape(seg_len, heads_local, DK)
    reduced_values = (
        plain_dot(a_all, wv_full).astype(jnp.bfloat16).reshape(seg_len, heads_local, DV)
    )
    gate_pre = plain_dot(a_all, wg_full)
    cosine, sine_tab, grow_fac = xpos_tables(positions, 1.0)
    _, _, shrink = xpos_tables(positions, -1.0)
    q_scale = DK ** (-0.5)
    rotated_queries = (rotate_pairs(queries, cosine, sine_tab, grow_fac) * q_scale).astype(
        jnp.bfloat16
    )
    rotated_keys = rotate_pairs(keys_raw, cosine, sine_tab, shrink).astype(jnp.bfloat16)
    local_state = jnp.einsum(
        "jld,jla->lda",
        rotated_keys.astype(jnp.float32) * state_weighting[:, :, None],
        reduced_values.astype(jnp.float32),
        precision=lax.Precision.HIGHEST,
    )
    slots = group_onehot[:, None, None, None] * (prompt_flag * local_state)[None]
    summed = lax.psum(slots, "dp")
    state_lookup = jnp.sum(summed * group_onehot[:, None, None, None], axis=0).astype(jnp.bfloat16)
    scores = jnp.einsum(
        "thk,nhk->htn", rotated_queries, rotated_keys, preferred_element_type=jnp.float32
    )
    weights_low = (scores * decay_mat).astype(jnp.bfloat16)
    retained_output = jnp.einsum(
        "htn,nhv->thv", weights_low, reduced_values, preferred_element_type=jnp.float32
    )
    carried_forward = jnp.einsum(
        "ozi,ziw->ozw", rotated_queries, state_lookup, preferred_element_type=jnp.float32
    )
    retained_output = retained_output + continuation_factor[:, :, None] * carried_forward
    grouped, inv_group = norm_stats(retained_output, GROUP_EPSILON)
    gate_act = jax.nn.silu(gate_pre).reshape(seg_len, heads_local, DV)
    gated_out = (gate_act * grouped).reshape(seg_len, heads_local * DV).astype(jnp.bfloat16)
    attn_own = scatter_rows(contract_last(gated_out, wo_full))
    hidden_res = token_rows + attn_own
    normed_two, inv_two = norm_stats(hidden_res, EPSILON)
    c_all = gather_rows((normed_two * gain_two + bias_two).astype(jnp.bfloat16))
    up_pre = plain_dot(c_all, wu_full)
    up_act = jax.nn.gelu(up_pre, approximate=False).astype(jnp.bfloat16)
    ffn_own = scatter_rows(contract_last(up_act, wd_full))
    block_out = hidden_res + ffn_own
    error_rows = block_out - teacher.astype(jnp.float32)
    weighted = loss_mask[:, None] * error_rows
    valid_count, squared = lax.psum(
        (jnp.sum(loss_mask), jnp.sum(weighted * error_rows)), ("dp", "mp")
    )
    grad_out = token_total / valid_count * weighted
    loss_value = squared / (valid_count * model_dim)
    grad_ffn_all = gather_rows(grad_out.astype(jnp.bfloat16))
    grad_up_act = plain_dot(grad_ffn_all, wd_full)
    _, gelu_pull = jax.vjp(lambda inner: jax.nn.gelu(inner, approximate=False), up_pre)
    grad_up = gelu_pull(grad_up_act)[0].astype(jnp.bfloat16)
    grad_wd = contract_first(grad_ffn_all, up_act)
    grad_wu = contract_first(c_all, grad_up)
    grad_c = scatter_rows(contract_last(grad_up, wu_full))
    grad_gain2_part = jnp.sum(grad_c * normed_two, axis=0)
    grad_bias2_part = jnp.sum(grad_c, axis=0)
    grad_hidden = grad_out + norm_back(grad_c * gain_two, normed_two, inv_two)
    ffn_reduced = (
        lax.psum_scatter(grad_gain2_part, "dp", scatter_dimension=0, tiled=True),
        lax.psum_scatter(grad_bias2_part, "dp", scatter_dimension=0, tiled=True),
        lax.psum_scatter(grad_wu, "dp", scatter_dimension=0, tiled=True),
        lax.psum_scatter(grad_wd, "dp", scatter_dimension=0, tiled=True),
    )
    grad_attn_all = gather_rows(grad_hidden.astype(jnp.bfloat16))
    grad_gated = plain_dot(grad_attn_all, wo_full).reshape(seg_len, heads_local, DV)
    grad_wo = contract_first(grad_attn_all, gated_out)
    _, silu_pull = jax.vjp(jax.nn.silu, gate_pre)
    grad_gate = silu_pull((grad_gated * grouped).reshape(seg_len, heads_local * DV))[0].astype(
        jnp.bfloat16
    )
    retained_gradient = norm_back(grad_gated * gate_act, grouped, inv_group).astype(jnp.bfloat16)
    grad_weights = jnp.einsum(
        "thv,nhv->htn", retained_gradient, reduced_values, preferred_element_type=jnp.float32
    )
    grad_values = jnp.einsum(
        "htn,thv->nhv", weights_low, retained_gradient, preferred_element_type=jnp.float32
    )
    grad_scores = (grad_weights * decay_mat).astype(jnp.bfloat16)
    grad_q_rot = jnp.einsum(
        "htn,nhk->thk", grad_scores, rotated_keys, preferred_element_type=jnp.float32
    )
    grad_q_rot = grad_q_rot + continuation_factor[:, :, None] * jnp.einsum(
        "mjr,jwr->mjw", retained_gradient, state_lookup, preferred_element_type=jnp.float32
    )
    grad_k_rot = jnp.einsum(
        "htn,thk->nhk", grad_scores, rotated_queries, preferred_element_type=jnp.float32
    )
    state_grad_own = jnp.einsum(
        "ybn,ybw->bnw",
        rotated_queries.astype(jnp.float32) * continuation_factor[:, :, None],
        retained_gradient.astype(jnp.float32),
        precision=lax.Precision.HIGHEST,
    )
    grad_slots = group_onehot[:, None, None, None] * state_grad_own[None]
    grad_summed = lax.psum(grad_slots, "dp")
    state_gradient = (
        prompt_flag * jnp.sum(grad_summed * group_onehot[:, None, None, None], axis=0)
    ).astype(jnp.bfloat16)
    grad_k_rot = grad_k_rot + state_weighting[:, :, None] * jnp.einsum(
        "ilm,lpm->ilp", reduced_values, state_gradient, preferred_element_type=jnp.float32
    )
    grad_values = grad_values + state_weighting[:, :, None] * jnp.einsum(
        "zdo,doi->zdi", rotated_keys, state_gradient, preferred_element_type=jnp.float32
    )
    grad_queries = (
        rotate_back(grad_q_rot * q_scale, cosine, sine_tab, grow_fac)
        .reshape(seg_len, heads_local * DK)
        .astype(jnp.bfloat16)
    )
    grad_keys = (
        rotate_back(grad_k_rot, cosine, sine_tab, shrink)
        .reshape(seg_len, heads_local * DK)
        .astype(jnp.bfloat16)
    )
    grad_vlow = grad_values.reshape(seg_len, heads_local * DV).astype(jnp.bfloat16)
    grad_wq = contract_first(a_all, grad_queries)
    grad_wk = contract_first(a_all, grad_keys)
    grad_wv = contract_first(a_all, grad_vlow)
    grad_wg = contract_first(a_all, grad_gate)
    grad_a_terms = (
        contract_last(grad_queries, wq_full)
        + contract_last(grad_keys, wk_full)
        + contract_last(grad_vlow, wv_full)
        + contract_last(grad_gate, wg_full)
    )
    grad_a = scatter_rows(grad_a_terms)
    grad_gain1_part = jnp.sum(grad_a * normed_one, axis=0)
    grad_bias1_part = jnp.sum(grad_a, axis=0)
    grad_tokens = grad_hidden + norm_back(grad_a * gain_one, normed_one, inv_one)
    attn_reduced = (
        lax.psum_scatter(grad_gain1_part, "dp", scatter_dimension=0, tiled=True),
        lax.psum_scatter(grad_bias1_part, "dp", scatter_dimension=0, tiled=True),
        lax.psum_scatter(grad_wq, "dp", scatter_dimension=0, tiled=True),
        lax.psum_scatter(grad_wk, "dp", scatter_dimension=0, tiled=True),
        lax.psum_scatter(grad_wv, "dp", scatter_dimension=0, tiled=True),
        lax.psum_scatter(grad_wg, "dp", scatter_dimension=0, tiled=True),
        lax.psum_scatter(grad_wo, "dp", scatter_dimension=0, tiled=True),
    )
    norm_sums = lax.psum((attn_reduced[0], attn_reduced[1], ffn_reduced[0], ffn_reduced[1]), "mp")
    return (
        block_out,
        grad_tokens,
        loss_value,
        norm_sums[0],
        norm_sums[1],
        attn_reduced[2],
        attn_reduced[3],
        attn_reduced[4],
        attn_reduced[5],
        attn_reduced[6],
        norm_sums[2],
        norm_sums[3],
        ffn_reduced[2],
        ffn_reduced[3],
    )


def solution(mesh):
    return jax.shard_map(
        on_device,
        mesh=mesh,
        in_specs=(
            P(("dp", "mp"), None),
            P(("dp", "mp"), None),
            P("dp", "mp"),
            P(),
            P(),
            P("dp"),
            P("dp"),
            P("dp", "mp"),
            P("dp", "mp"),
            P("dp", "mp"),
            P("dp", "mp"),
            P("dp", "mp"),
            P("dp"),
            P("dp"),
            P("dp", "mp"),
            P("dp", "mp"),
        ),
        out_specs=(
            P(("dp", "mp"), None),
            P(("dp", "mp"), None),
            P(),
            P("dp"),
            P("dp"),
            P("dp", "mp"),
            P("dp", "mp"),
            P("dp", "mp"),
            P("dp", "mp"),
            P("dp", "mp"),
            P("dp"),
            P("dp"),
            P("dp", "mp"),
            P("dp", "mp"),
        ),
        check_vma=False,
    )
```

profile of v0, /device:TPU:0, one launch (start us, length us, event | category | flops | bytes accessed | tf_op | source)
XLA Modules:
  0.0 2218.7 jit_solution(17705684298100000474)
XLA Ops:
  9.8 23.3 %all-gather = bf16[16,1,128]{2,1,0:T(2,128)(2,1)S(1)} all-gather(bf16[1,1,128]{2,1,0:T(2,128)(2,1)} %bitcast.140), channel_id=1, replica_groups=mesh['dp'=16,'mp'=2] {'dp'}, dimensions={0}, use_global_device_ids=true | all-gather | bytes 4352 | tf_op jit(solution)/shard_map/all_gather | solution.py:120
  33.1 17.6 all-gather.1
  64.5 8.4 all-gather.16.cloned.1.call-done
  72.8 52.6 %all-gather.24.cloned.1.call-done = bf16[2048,1024]{1,0:T(8,128)(2,1)} async-done(((bf16[128,1024]{1,0:T(8,128)(2,1)}), bf16[2048,1024]{1,0:T(8,128)(2,1)}) %all-gather.24.cloned.1.call-update) | async-done | bytes 4194320 | tf_op jit(solution)/shard_map/all_gather | solution.py:123
  125.4 3.8 fusion.70
  129.7 46.8 %all-gather.22.cloned.1.call-done = bf16[2048,1024]{1,0:T(8,128)(2,1)} async-done(((bf16[128,1024]{1,0:T(8,128)(2,1)}), bf16[2048,1024]{1,0:T(8,128)(2,1)}) %all-gather.22.cloned.1.call-update) | async-done | bytes 4194320 | tf_op jit(solution)/shard_map/all_gather | solution.py:122
  176.5 4.4 fusion.69
  185.0 66.4 %all-gather.20.cloned.1.call-done = bf16[2048,2048]{1,0:T(8,128)(2,1)} async-done(((bf16[128,2048]{1,0:T(8,128)(2,1)}), bf16[2048,2048]{1,0:T(8,128)(2,1)}) %all-gather.20.cloned.1.call-update) | async-done | bytes 8388624 | tf_op jit(solution)/shard_map/all_gather | solution.py:124
  251.4 5.7 convolution_convert_fusion
  265.3 61.1 %all-gather.18.cloned.1.call-done = bf16[2048,2048]{1,0:T(8,128)(2,1)} async-done(((bf16[128,2048]{1,0:T(8,128)(2,1)}), bf16[2048,2048]{1,0:T(8,128)(2,1)}) %all-gather.18.cloned.1.call-update) | async-done | bytes 8388624 | tf_op jit(solution)/shard_map/all_gather | solution.py:125
  326.3 7.8 fusion.12
  339.0 100.7 %all-reduce.10.cloned.1.call-done = f32[2,4,256,512]{3,2,1,0:T(8,128)} async-done(((f32[2,4,256,512]{3,2,1,0:T(8,128)}), f32[2,4,256,512]{3,2,1,0:T(8,128)}) %all-reduce.10.cloned.1.call-update) | async-done | bytes 4194320 | tf_op jit(solution)/shard_map/psum | solution.py:204
  445.8 69.5 %all-gather.26.cloned.1.call-done = bf16[2048,2048]{1,0:T(8,128)(2,1)} async-done(((bf16[128,2048]{1,0:T(8,128)(2,1)}), bf16[2048,2048]{1,0:T(8,128)(2,1)}) %all-gather.26.cloned.1.call-update) | async-done | bytes 8388624 | tf_op jit(solution)/shard_map/all_gather | solution.py:126
  515.3 7.1 fusion.71
  523.2 19.0 all-gather.2
  542.2 17.4 all-gather.3
  564.7 64.9 %all-gather.30.cloned.1.call-done = bf16[2048,2048]{1,0:T(8,128)(2,1)} async-done(((bf16[128,2048]{1,0:T(8,128)(2,1)}), bf16[2048,2048]{1,0:T(8,128)(2,1)}) %all-gather.30.cloned.1.call-update) | async-done | bytes 8388624 | tf_op jit(solution)/shard_map/all_gather | solution.py:131
  629.6 21.9 all-gather.28.cloned.1.call-done
  651.4 10.6 multiply_convert_fusion.2
  662.1 65.9 %all-gather.32.cloned.1.call-done = bf16[2048,2048]{1,0:T(8,128)(2,1)} async-done(((bf16[128,2048]{1,0:T(8,128)(2,1)}), bf16[2048,2048]{1,0:T(8,128)(2,1)}) %all-gather.32.cloned.1.call-update) | async-done | bytes 8388624 | tf_op jit(solution)/shard_map/all_gather | solution.py:132
  727.9 7.4 fusion.72
  737.8 28.2 %reduce-scatter.14.cloned.1.call-done = f32[128,2048]{1,0:T(8,128)} async-done(((f32[256,2048]{1,0:T(8,128)}), f32[128,2048]{1,0:T(8,128)}) %reduce-scatter.14.cloned.1.call-update) | async-done | bytes 1048592 | tf_op jit(solution)/shard_map/reduce_scatter | solution.py:89
  769.2 39.5 %all-reduce.4 = (f32[]{:T(128)}, f32[]{:T(128)}) all-reduce(f32[]{:T(128)} %get-tuple-element.39, f32[]{:T(128)} %get-tuple-element.37), channel_id=1, replica_groups=mesh['dp'=16,'mp'=2] {'dp','mp'}, use_global_device_ids=true, to_apply=%region_14.15 | all-reduce | flops 2 | bytes 16 | tf_op jit(solution)/shard_map/psum | solution.py:230
  811.9 22.3 %all-gather.34.cloned.1.call-done = bf16[256,2048]{1,0:T(8,128)(2,1)} async-done(((bf16[128,2048]{1,0:T(8,128)(2,1)}), bf16[256,2048]{1,0:T(8,128)(2,1)}) %all-gather.34.cloned.1.call-update) | async-done | bytes 1048592 | tf_op jit(solution)/shard_map/all_gather | solution.py:85
  834.2 7.7 add_convert_fusion
  842.9 7.1 fusion.73
  850.2 31.8 %reduce-scatter.16.cloned.1.call-done = f32[128,2048]{1,0:T(8,128)} async-done(((f32[256,2048]{1,0:T(8,128)}), f32[128,2048]{1,0:T(8,128)}) %reduce-scatter.16.cloned.1.call-update) | async-done | bytes 1048592 | tf_op jit(solution)/shard_map/reduce_scatter | solution.py:89
  887.6 21.4 all-gather.36.cloned.1.call-done
  909.0 7.2 fusion.74
  936.8 98.4 %all-reduce.12.cloned.1.call-done = f32[2,4,256,512]{3,2,1,0:T(8,128)} async-done(((f32[2,4,256,512]{3,2,1,0:T(8,128)}), f32[2,4,256,512]{3,2,1,0:T(8,128)}) %all-reduce.12.cloned.1.call-update) | async-done | bytes 4194320 | tf_op jit(solution)/shard_map/psum | solution.py:282
  1042.0 3.6 fusion.75
  1047.0 6.0 convolution_add_fusion.2
  1053.0 3.9 convolution_add_fusion.1
  1058.1 4.8 fusion.78
  1063.0 4.6 fusion.77
  1068.9 9.4 fusion.82
  1079.5 9.4 fusion.83
  1090.0 9.8 fusion.81
  1100.2 9.8 fusion.80
  1111.3 8.1 fusion.79
  1124.5 62.8 %all-reduce.5 = (f32[2048]{0:T(1024)S(1)}, f32[2048]{0:T(1024)S(1)}, f32[2048]{0:T(1024)S(1)}, f32[2048]{0:T(1024)S(1)}) all-reduce(f32[2048]{0:T(1024)S(1)} %get-tuple-element.18, f32[2048]{0:T(1024)S(1)} %get-tuple-element.23, f32[2048]{0:T(1024)S(1)} %copy-done.51, ...), channel_id=6, replica_groups=mesh['dp'=16,'mp'=2] {'dp'}, use_global_device_ids=true, to_apply=%region_28.29.clone | all-reduce | flops 8192 | bytes 65536
  1187.6 5.4 all-reduce.6
  1196.8 107.8 %reduce-scatter.20.cloned.1.call-done = f32[128,1024]{1,0:T(8,128)} async-done(((f32[2048,1024]{1,0:T(8,128)}), f32[128,1024]{1,0:T(8,128)}) %reduce-scatter.20.cloned.1.call-update) | async-done | bytes 524304 | tf_op jit(solution)/shard_map/reduce_scatter | solution.py:320
  1304.6 181.5 %reduce-scatter.30.cloned.1.call-done = f32[128,2048]{1,0:T(8,128)} async-done(((f32[2048,2048]{1,0:T(8,128)}), f32[128,2048]{1,0:T(8,128)}) %reduce-scatter.30.cloned.1.call-update) | async-done | bytes 1048592 | tf_op jit(solution)/shard_map/reduce_scatter | solution.py:248
  1486.1 181.1 %reduce-scatter.32.cloned.1.call-done = f32[128,2048]{1,0:T(8,128)} async-done(((f32[2048,2048]{1,0:T(8,128)}), f32[128,2048]{1,0:T(8,128)}) %reduce-scatter.32.cloned.1.call-update) | async-done | bytes 1048592 | tf_op jit(solution)/shard_map/reduce_scatter | solution.py:249
  1667.3 181.1 %reduce-scatter.28.cloned.1.call-done = f32[128,2048]{1,0:T(8,128)} async-done(((f32[2048,2048]{1,0:T(8,128)}), f32[128,2048]{1,0:T(8,128)}) %reduce-scatter.28.cloned.1.call-update) | async-done | bytes 1048592 | tf_op jit(solution)/shard_map/reduce_scatter | solution.py:324
  1848.4 181.1 %reduce-scatter.26.cloned.1.call-done = f32[128,2048]{1,0:T(8,128)} async-done(((f32[2048,2048]{1,0:T(8,128)}), f32[128,2048]{1,0:T(8,128)}) %reduce-scatter.26.cloned.1.call-update) | async-done | bytes 1048592 | tf_op jit(solution)/shard_map/reduce_scatter | solution.py:323
  2029.5 181.0 %reduce-scatter.24.cloned.1.call-done = f32[128,2048]{1,0:T(8,128)} async-done(((f32[2048,2048]{1,0:T(8,128)}), f32[128,2048]{1,0:T(8,128)}) %reduce-scatter.24.cloned.1.call-update) | async-done | bytes 1048592 | tf_op jit(solution)/shard_map/reduce_scatter | solution.py:322
  (283 shorter events, 100.2 us)
Async XLA Ops:
  7.2 48.6 %copy-start.68 = (s32[16]{0:T(128)S(1)}, s32[16]{0:T(128)}, u32[]{:S(2)}) copy-start(s32[16]{0:T(128)} %param.19) | copy-start | bytes 196
  7.2 51.2 %copy-start.69 = (s32[2]{0:T(128)S(1)}, s32[2]{0:T(128)}, u32[]{:S(2)}) copy-start(s32[2]{0:T(128)} %param.20) | copy-start | bytes 28
  7.2 65.6 %all-gather.16.cloned.1.call-start = ((), (), s32[]{:S(2)}) async-start(), calls=%async_computation.11 | async-start | bytes 1572864 | tf_op jit(solution)/shard_map/all_gather | solution.py:85
  8.4 42.3 %copy-start.53 = (f32[128]{0:T(128)}, f32[128]{0:T(128)S(1)}, u32[]{:S(2)}) copy-start(f32[128]{0:T(128)S(1)} %broadcast_multiply_fusion.10) | copy-start | bytes 1540
  9.8 41.0 %copy-start.60 = (f32[128]{0:T(128)}, f32[128]{0:T(128)S(1)}, u32[]{:S(2)}) copy-start(f32[128]{0:T(128)S(1)} %add_rsqrt_fusion.2) | copy-start | bytes 1540
  33.1 17.7 copy-start.43
  53.1 72.4 %all-gather.24.cloned.1.call-start = ((), (), s32[]{:S(2)}) async-start(), calls=%async_computation.15 | async-start | bytes 4456448 | tf_op jit(solution)/shard_map/all_gather | solution.py:123
  53.8 122.7 %all-gather.22.cloned.1.call-start = ((), (), s32[]{:S(2)}) async-start(), calls=%async_computation.14 | async-start | bytes 4456448 | tf_op jit(solution)/shard_map/all_gather | solution.py:122
  54.5 196.9 %all-gather.20.cloned.1.call-start = ((), (), s32[]{:S(2)}) async-start(), calls=%async_computation.13 | async-start | bytes 8912896 | tf_op jit(solution)/shard_map/all_gather | solution.py:124
  55.1 271.2 %all-gather.18.cloned.1.call-start = ((), (), s32[]{:S(2)}) async-start(), calls=%async_computation.12 | async-start | bytes 8912896 | tf_op jit(solution)/shard_map/all_gather | solution.py:125
  55.7 384.0 %all-reduce.10.cloned.1.call-start = ((), (), s32[]{:S(2)}) async-start(), calls=%async_computation.16 | async-start | bytes 8388608 | tf_op jit(solution)/shard_map/psum | solution.py:204
  61.6 378.1 %copy-start.57 = (f32[2]{0:T(128)}, f32[2]{0:T(128)S(1)}, u32[]{:S(2)}) copy-start(f32[2]{0:T(128)S(1)} %compare_convert_fusion) | copy-start | bytes 28
  62.3 201.7 %copy-start.66 = (f32[4]{0:T(128)}, f32[4]{0:T(128)S(1)}, u32[]{:S(2)}) copy-start(f32[4]{0:T(128)S(1)} %subtract_log_fusion) | copy-start | bytes 52
  62.4 194.7 %copy-start.46 = (f32[256,4]{0,1:T(4,128)}, f32[256,4]{0,1:T(4,128)S(1)}, u32[]{:S(2)}) copy-start(f32[256,4]{0,1:T(4,128)S(1)} %get-tuple-element.64) | copy-start | bytes 12292
  62.4 380.3 %copy-start.48 = (f32[256,4]{0,1:T(4,128)}, f32[256,4]{0,1:T(4,128)S(1)}, u32[]{:S(2)}) copy-start(f32[256,4]{0,1:T(4,128)S(1)} %get-tuple-element.65) | copy-start | bytes 12292
  129.2 47.4 %copy-start = (bf16[256,2048]{1,0:T(8,128)(2,1)S(1)}, bf16[256,2048]{1,0:T(8,128)(2,1)}, u32[]{:S(2)}) copy-start(bf16[256,2048]{1,0:T(8,128)(2,1)} %all-gather.16.cloned.1.call-done) | copy-start | bytes 3145732
  185.0 79.1 %copy-start.27 = (bf16[256,4,128]{2,0,1:T(8,128)(2,1)}, bf16[256,4,128]{2,0,1:T(8,128)(2,1)S(1)}, u32[]{:S(2)}) copy-start(bf16[256,4,128]{2,0,1:T(8,128)(2,1)S(1)} %get-tuple-element.51) | copy-start | bytes 786436
  257.1 80.0 %copy-start.5 = (bf16[256,2048]{1,0:T(8,128)(2,1)}, bf16[256,2048]{1,0:T(8,128)(2,1)S(1)}, u32[]{:S(2)}) copy-start(bf16[256,2048]{1,0:T(8,128)(2,1)S(1)} %convolution_convert_fusion) | copy-start | bytes 3145732
  261.1 254.1 %all-gather.26.cloned.1.call-start = ((), (), s32[]{:S(2)}) async-start(), calls=%async_computation.17 | async-start | bytes 8912896 | tf_op jit(solution)/shard_map/all_gather | solution.py:126
  261.9 298.4 %reduce-scatter.12.cloned.1.call-start = ((), (), s32[]{:S(2)}) async-start(), calls=%async_computation.18 | async-start | bytes 3145728 | tf_op jit(solution)/shard_map/reduce_scatter | solution.py:89
  264.1 178.7 %copy-start.13 = (bf16[256,4,256]{2,0,1:T(8,128)(2,1)}, bf16[256,4,256]{2,0,1:T(8,128)(2,1)S(1)}, u32[]{:S(2)}) copy-start(bf16[256,4,256]{2,0,1:T(8,128)(2,1)S(1)} %fusion.41) | copy-start | bytes 1572868
  445.8 76.6 %copy-start.17 = (bf16[256,4,512]{0,2,1:T(8,128)(2,1)}, bf16[256,4,512]{0,2,1:T(8,128)(2,1)S(1)}, u32[]{:S(2)}) copy-start(bf16[256,4,512]{0,2,1:T(8,128)(2,1)S(1)} %multiply_convert_fusion.3) | copy-start | bytes 3145732
  522.4 19.8 copy-start.65
  522.4 107.2 %all-gather.30.cloned.1.call-start = ((), (), s32[]{:S(2)}) async-start(), calls=%async_computation.20 | async-start | bytes 8912896 | tf_op jit(solution)/shard_map/all_gather | solution.py:131
  523.2 128.3 %all-gather.28.cloned.1.call-start = ((), (), s32[]{:S(2)}) async-start(), calls=%async_computation.19 | async-start | bytes 1572864 | tf_op jit(solution)/shard_map/all_gather | solution.py:85
  563.7 164.2 %all-gather.32.cloned.1.call-start = ((), (), s32[]{:S(2)}) async-start(), calls=%async_computation.21 | async-start | bytes 8912896 | tf_op jit(solution)/shard_map/all_gather | solution.py:132
  564.5 201.6 %reduce-scatter.14.cloned.1.call-start = ((), (), s32[]{:S(2)}) async-start(), calls=%async_computation.22 | async-start | bytes 3145728 | tf_op jit(solution)/shard_map/reduce_scatter | solution.py:89
  735.4 98.8 %all-gather.34.cloned.1.call-start = ((), (), s32[]{:S(2)}) async-start(), calls=%async_computation.23 | async-start | bytes 1572864 | tf_op jit(solution)/shard_map/all_gather | solution.py:85
  811.8 70.2 %reduce-scatter.16.cloned.1.call-start = ((), (), s32[]{:S(2)}) async-start(), calls=%async_computation.24 | async-start | bytes 3145728 | tf_op jit(solution)/shard_map/reduce_scatter | solution.py:89
  850.0 59.0 %all-gather.36.cloned.1.call-start = ((), (), s32[]{:S(2)}) async-start(), calls=%async_computation.25 | async-start | bytes 1572864 | tf_op jit(solution)/shard_map/all_gather | solution.py:85
  887.6 147.5 %all-reduce.12.cloned.1.call-start = ((), (), s32[]{:S(2)}) async-start(), calls=%async_computation.26 | async-start | bytes 8388608 | tf_op jit(solution)/shard_map/psum | solution.py:282
  909.0 7.2 copy-start.3
  923.8 198.8 %reduce-scatter.18.cloned.1.call-start = ((), (), s32[]{:S(2)}) async-start(), calls=%async_computation.27 | async-start | bytes 3145728 | tf_op jit(solution)/shard_map/reduce_scatter | solution.py:89
  936.7 101.4 %copy-start.12 = (f32[4,512,256]{2,1,0:T(8,128)S(1)}, f32[4,512,256]{2,1,0:T(8,128)}, u32[]{:S(2)}) copy-start(f32[4,512,256]{2,1,0:T(8,128)} %fusion.76) | copy-start | bytes 6291460
  936.7 101.4 %copy-start.47 = (f32[256,4]{0,1:T(4,128)S(1)}, f32[256,4]{0,1:T(4,128)}, u32[]{:S(2)}) copy-start(f32[256,4]{0,1:T(4,128)} %copy-done.46) | copy-start | bytes 12292
  1045.6 7.4 slice-start
  1047.0 6.0 copy-start.19
  1047.0 6.0 slice-start.1
  1056.9 139.8 %reduce-scatter.22.cloned.1.call-start = ((), (), s32[]{:S(2)}) async-start(), calls=%async_computation.29 | async-start | bytes 8912896 | tf_op jit(solution)/shard_map/reduce_scatter | solution.py:321
  1063.0 241.6 %reduce-scatter.20.cloned.1.call-start = ((), (), s32[]{:S(2)}) async-start(), calls=%async_computation.28 | async-start | bytes 8912896 | tf_op jit(solution)/shard_map/reduce_scatter | solution.py:320
  1067.7 418.4 %reduce-scatter.30.cloned.1.call-start = ((), (), s32[]{:S(2)}) async-start(), calls=%async_computation.33 | async-start | bytes 17825792 | tf_op jit(solution)/shard_map/reduce_scatter | solution.py:248
  1078.3 589.0 %reduce-scatter.32.cloned.1.call-start = ((), (), s32[]{:S(2)}) async-start(), calls=%async_computation.34 | async-start | bytes 17825792 | tf_op jit(solution)/shard_map/reduce_scatter | solution.py:249
  1088.9 759.5 %reduce-scatter.28.cloned.1.call-start = ((), (), s32[]{:S(2)}) async-start(), calls=%async_computation.32 | async-start | bytes 17825792 | tf_op jit(solution)/shard_map/reduce_scatter | solution.py:324
  1099.9 929.6 %reduce-scatter.26.cloned.1.call-start = ((), (), s32[]{:S(2)}) async-start(), calls=%async_computation.31 | async-start | bytes 17825792 | tf_op jit(solution)/shard_map/reduce_scatter | solution.py:323
  1110.0 1100.5 %reduce-scatter.24.cloned.1.call-start = ((), (), s32[]{:S(2)}) async-start(), calls=%async_computation.30 | async-start | bytes 17825792 | tf_op jit(solution)/shard_map/reduce_scatter | solution.py:322
  1119.4 5.0 copy-start.51
  1119.5 73.6 %copy-start.23 = (f32[128,2048]{1,0:T(8,128)S(1)}, f32[128,2048]{1,0:T(8,128)}, u32[]{:S(2)}) copy-start(f32[128,2048]{1,0:T(8,128)} %get-tuple-element.36) | copy-start | bytes 3145732
  1122.7 70.4 %copy-start.21 = (f32[128,2048]{1,0:T(8,128)S(1)}, f32[128,2048]{1,0:T(8,128)}, u32[]{:S(2)}) copy-start(f32[128,2048]{1,0:T(8,128)} %reduce-scatter.18.cloned.1.call-done) | copy-start | bytes 3145732
  (49 other events, 95.6 us)
Sparse Core Ops, SparseCore 0:
  53.2 19.6 all-gather.15
  75.0 50.3 all-gather.23
  127.6 48.8 all-gather.21
  178.5 72.8 all-gather.19
  253.4 72.8 all-gather.17
  329.9 109.7 all-reduce.9
  441.8 73.4 all-gather.25
  522.5 30.4 reduce-scatter.11
  555.2 74.3 all-gather.29
  631.5 19.8 all-gather.27
  653.6 74.2 all-gather.31
  735.5 30.4 reduce-scatter.13
  812.0 22.1 all-gather.33
  850.1 31.8 reduce-scatter.15
  887.7 21.2 all-gather.35
  924.0 111.1 all-reduce.11
  1057.1 31.0 reduce-scatter.17
  1092.6 104.1 reduce-scatter.21
  1201.4 103.1 reduce-scatter.19
  1309.1 176.9 reduce-scatter.29
  1490.8 176.4 reduce-scatter.31
  1671.9 176.3 reduce-scatter.27
  1853.1 176.3 reduce-scatter.25
  2034.0 176.3 reduce-scatter.23
where the time goes:
time: 2230 us; the launch traced here: 2220 us
  waiting for transfers between devices  1780 us (80%)
  blocking collectives  185 us (8%)
  matrix products  155 us (7%)
  other arithmetic  51.2 us (2%)
  local copies, waits for them, and re-layouts  23 us (1%)
    reduce_scatter x1, waiting for transfers between devices, on_device(): lax.psum_scatter(grad_wu, 'dp', scatter_dimension=0, tiled=True)  182 us
    reduce_scatter x1, waiting for transfers between devices, on_device(): lax.psum_scatter(grad_wd, 'dp', scatter_dimension=0, tiled=True)  181 us
    reduce_scatter x1, waiting for transfers between devices, on_device(): lax.psum_scatter(grad_wg, 'dp', scatter_dimension=0, tiled=True)  181 us
    reduce_scatter x1, waiting for transfers between devices, on_device(): lax.psum_scatter(grad_wo, 'dp', scatter_dimension=0, tiled=True)  181 us
    reduce_scatter x1, waiting for transfers between devices, on_device(): lax.psum_scatter(grad_wv, 'dp', scatter_dimension=0, tiled=True)  181 us
    reduce_scatter x1, waiting for transfers between devices, on_device(): lax.psum_scatter(grad_wq, 'dp', scatter_dimension=0, tiled=True)  108 us
    psum x1, waiting for transfers between devices, on_device(): summed = lax.psum(slots, 'dp')  101 us
    psum x1, waiting for transfers between devices, on_device(): grad_summed = lax.psum(grad_slots, 'dp')  98.4 us
  transfers between devices with their start and end apart: 24, of which 22 were waited for; matrix products, arithmetic and copies ran while one was open for 6% of the time, Pallas kernels for 0%

commit v1 on v0

--- a/solution.py
+++ b/solution.py
@@ -279,7 +279,11 @@
         precision=lax.Precision.HIGHEST,
     )
     grad_slots = group_onehot[:, None, None, None] * state_grad_own[None]
-    grad_summed = lax.psum(grad_slots, "dp")
+    grad_summed = grad_slots
+    for hop in (1, 2, 4, 8):
+        grad_summed = grad_summed + lax.ppermute(
+            grad_summed, "dp", [(dev, dev ^ hop) for dev in range(16)]
+        )
     state_gradient = (
         prompt_flag * jnp.sum(grad_summed * group_onehot[:, None, None, None], axis=0)
     ).astype(jnp.bfloat16)

time: 2230 us -> 2490 us (1.12)
  waiting for transfers between devices: 1780 us -> 2040 us
    ppermute x0 -> x4, waiting for transfers between devices: none -> 358 us  [on_device(): lax.ppermute(grad_summed, 'dp', [(dev, dev ^ hop) for dev in range(16)])]
    reduce_scatter x1, waiting for transfers between devices: 182 us -> 71 us  [on_device(): lax.psum_scatter(grad_wu, 'dp', scatter_dimension=0, tiled=True)]
    reduce_scatter x1, waiting for transfers between devices: 2.26 us -> 107 us  [on_device(): lax.psum_scatter(grad_wk, 'dp', scatter_dimension=0, tiled=True)]
    psum x1 -> x0, waiting for transfers between devices: 98.4 us -> none  [on_device(): grad_summed = lax.psum(grad_slots, 'dp')]
  transfers between devices with their start and end apart: 24 -> 27, of which waited for: 22 -> 25; matrix products, arithmetic and copies ran while one was open for 6% -> 5% of each run, Pallas kernels for 0% -> 0%
where the time goes in v1:
time: 2490 us
  waiting for transfers between devices  2040 us (82%)
  blocking collectives  188 us (8%)
  matrix products  155 us (6%)
  other arithmetic  55.6 us (2%)
    ppermute x4, waiting for transfers between devices, on_device(): lax.ppermute(grad_summed, 'dp', [(dev, dev ^ hop) for dev in range(16)])  358 us
    reduce_scatter x1, waiting for transfers between devices, on_device(): lax.psum_scatter(grad_wv, 'dp', scatter_dimension=0, tiled=True)  182 us
    reduce_scatter x1, waiting for transfers between devices, on_device(): lax.psum_scatter(grad_wo, 'dp', scatter_dimension=0, tiled=True)  181 us
    reduce_scatter x1, waiting for transfers between devices, on_device(): lax.psum_scatter(grad_wd, 'dp', scatter_dimension=0, tiled=True)  181 us
    reduce_scatter x1, waiting for transfers between devices, on_device(): lax.psum_scatter(grad_wg, 'dp', scatter_dimension=0, tiled=True)  181 us
    reduce_scatter x1, waiting for transfers between devices, on_device(): lax.psum_scatter(grad_wq, 'dp', scatter_dimension=0, tiled=True)  108 us
    reduce_scatter x1, waiting for transfers between devices, on_device(): lax.psum_scatter(grad_wk, 'dp', scatter_dimension=0, tiled=True)  107 us
    psum x1, waiting for transfers between devices, on_device(): summed = lax.psum(slots, 'dp')  101 us
  transfers between devices with their start and end apart: 27, of which 25 were waited for; matrix products, arithmetic and copies ran while one was open for 5% of the time, Pallas kernels for 0%

profile of v1, /device:TPU:0, one launch (start us, length us, event | category | flops | bytes accessed | tf_op | source)
XLA Modules:
  0.0 2486.5 jit_solution(8708698166696597339)
XLA Ops:
  9.8 23.3 all-gather
  33.1 17.6 all-gather.1
  64.5 8.3 all-gather.16.cloned.1.call-done
  72.8 52.6 %all-gather.24.cloned.1.call-done = bf16[2048,1024]{1,0:T(8,128)(2,1)} async-done(((bf16[128,1024]{1,0:T(8,128)(2,1)}), bf16[2048,1024]{1,0:T(8,128)(2,1)}) %all-gather.24.cloned.1.call-update) | async-done | bytes 4194320 | tf_op jit(solution)/shard_map/all_gather | solution.py:123
  129.7 46.8 %all-gather.22.cloned.1.call-done = bf16[2048,1024]{1,0:T(8,128)(2,1)} async-done(((bf16[128,1024]{1,0:T(8,128)(2,1)}), bf16[2048,1024]{1,0:T(8,128)(2,1)}) %all-gather.22.cloned.1.call-update) | async-done | bytes 4194320 | tf_op jit(solution)/shard_map/all_gather | solution.py:122
  185.0 66.4 %all-gather.20.cloned.1.call-done = bf16[2048,2048]{1,0:T(8,128)(2,1)} async-done(((bf16[128,2048]{1,0:T(8,128)(2,1)}), bf16[2048,2048]{1,0:T(8,128)(2,1)}) %all-gather.20.cloned.1.call-update) | async-done | bytes 8388624 | tf_op jit(solution)/shard_map/all_gather | solution.py:124
  251.4 5.7 convolution_convert_fusion
  265.3 61.1 %all-gather.18.cloned.1.call-done = bf16[2048,2048]{1,0:T(8,128)(2,1)} async-done(((bf16[128,2048]{1,0:T(8,128)(2,1)}), bf16[2048,2048]{1,0:T(8,128)(2,1)}) %all-gather.18.cloned.1.call-update) | async-done | bytes 8388624 | tf_op jit(solution)/shard_map/all_gather | solution.py:125
  326.3 7.8 fusion.12
  339.0 100.7 %all-reduce.9.cloned.1.call-done = f32[2,4,256,512]{3,2,1,0:T(8,128)} async-done(((f32[2,4,256,512]{3,2,1,0:T(8,128)}), f32[2,4,256,512]{3,2,1,0:T(8,128)}) %all-reduce.9.cloned.1.call-update) | async-done | bytes 4194320 | tf_op jit(solution)/shard_map/psum | solution.py:204
  445.8 69.5 %all-gather.26.cloned.1.call-done = bf16[2048,2048]{1,0:T(8,128)(2,1)} async-done(((bf16[128,2048]{1,0:T(8,128)(2,1)}), bf16[2048,2048]{1,0:T(8,128)(2,1)}) %all-gather.26.cloned.1.call-update) | async-done | bytes 8388624 | tf_op jit(solution)/shard_map/all_gather | solution.py:126
  515.3 7.1 fusion.72
  523.2 19.0 all-gather.2
  542.2 17.4 all-gather.3
  564.7 64.9 %all-gather.30.cloned.1.call-done = bf16[2048,2048]{1,0:T(8,128)(2,1)} async-done(((bf16[128,2048]{1,0:T(8,128)(2,1)}), bf16[2048,2048]{1,0:T(8,128)(2,1)}) %all-gather.30.cloned.1.call-update) | async-done | bytes 8388624 | tf_op jit(solution)/shard_map/all_gather | solution.py:131
  629.6 21.9 all-gather.28.cloned.1.call-done
  651.4 10.6 multiply_convert_fusion.2
  662.0 65.9 %all-gather.32.cloned.1.call-done = bf16[2048,2048]{1,0:T(8,128)(2,1)} async-done(((bf16[128,2048]{1,0:T(8,128)(2,1)}), bf16[2048,2048]{1,0:T(8,128)(2,1)}) %all-gather.32.cloned.1.call-update) | async-done | bytes 8388624 | tf_op jit(solution)/shard_map/all_gather | solution.py:132
  727.9 7.4 fusion.73
  737.8 28.2 %reduce-scatter.14.cloned.1.call-done = f32[128,2048]{1,0:T(8,128)} async-done(((f32[256,2048]{1,0:T(8,128)}), f32[128,2048]{1,0:T(8,128)}) %reduce-scatter.14.cloned.1.call-update) | async-done | bytes 1048592 | tf_op jit(solution)/shard_map/reduce_scatter | solution.py:89
  769.2 39.5 %all-reduce.4 = (f32[]{:T(128)}, f32[]{:T(128)}) all-reduce(f32[]{:T(128)} %get-tuple-element.39, f32[]{:T(128)} %get-tuple-element.37), channel_id=1, replica_groups=mesh['dp'=16,'mp'=2] {'dp','mp'}, use_global_device_ids=true, to_apply=%region_14.15 | all-reduce | flops 2 | bytes 16 | tf_op jit(solution)/shard_map/psum | solution.py:230
  811.9 22.3 all-gather.34.cloned.1.call-done
  834.2 7.7 add_convert_fusion
  842.9 7.1 fusion.74
  850.2 31.8 %reduce-scatter.16.cloned.1.call-done = f32[128,2048]{1,0:T(8,128)} async-done(((f32[256,2048]{1,0:T(8,128)}), f32[128,2048]{1,0:T(8,128)}) %reduce-scatter.16.cloned.1.call-update) | async-done | bytes 1048592 | tf_op jit(solution)/shard_map/reduce_scatter | solution.py:89
  887.6 21.4 all-gather.36.cloned.1.call-done
  909.0 7.2 fusion.75
  922.0 7.1 collective-permute-done
  931.5 91.1 %collective-permute-done.1 = f32[2,4,256,512]{3,2,1,0:T(8,128)S(1)} collective-permute-done((f32[2,4,256,512]{3,2,1,0:T(8,128)S(1)}, f32[2,4,256,512]{3,2,1,0:T(8,128)S(1)}, u32[]{:S(2)}, u32[]{:S(2)}) %collective-permute-start.1) | collective-permute-done | bytes 4194336 | tf_op jit(solution)/shard_map/ppermute | solution.py:284
  1025.6 90.3 %collective-permute-done.2 = f32[2,4,256,512]{3,2,1,0:T(8,128)S(1)} collective-permute-done((f32[2,4,256,512]{3,2,1,0:T(8,128)S(1)}, f32[2,4,256,512]{3,2,1,0:T(8,128)S(1)}, u32[]{:S(2)}, u32[]{:S(2)}) %collective-permute-start.2) | collective-permute-done | bytes 4194336 | tf_op jit(solution)/shard_map/ppermute | solution.py:284
  1131.5 169.3 %collective-permute-done.3 = f32[2,4,256,512]{3,2,1,0:T(8,128)} collective-permute-done((f32[2,4,256,512]{3,2,1,0:T(8,128)}, f32[2,4,256,512]{3,2,1,0:T(8,128)}, u32[]{:S(2)}, u32[]{:S(2)}) %collective-permute-start.3) | collective-permute-done | bytes 4194336 | tf_op jit(solution)/shard_map/ppermute | solution.py:284
  1314.3 6.0 convolution_add_fusion.2
  1325.4 9.9 fusion.83
  1336.5 9.4 fusion.84
  1347.1 9.4 fusion.82
  1357.7 8.3 fusion.81
  1366.3 5.9 fusion.79
  1372.3 5.8 fusion.78
  1379.6 10.2 fusion.80
  1394.8 65.9 %all-reduce.5 = (f32[2048]{0:T(1024)S(1)}, f32[2048]{0:T(1024)S(1)}, f32[2048]{0:T(1024)S(1)}, f32[2048]{0:T(1024)S(1)}) all-reduce(f32[2048]{0:T(1024)S(1)} %get-tuple-element.18, f32[2048]{0:T(1024)S(1)} %get-tuple-element.23, f32[2048]{0:T(1024)S(1)} %copy-done.46, ...), channel_id=6, replica_groups=mesh['dp'=16,'mp'=2] {'dp'}, use_global_device_ids=true, to_apply=%region_27.28.clone | all-reduce | flops 8192 | bytes 65536
  1461.0 5.4 all-reduce.6
  1467.9 71.0 %reduce-scatter.30.cloned.1.call-done = f32[128,2048]{1,0:T(8,128)} async-done(((f32[2048,2048]{1,0:T(8,128)}), f32[128,2048]{1,0:T(8,128)}) %reduce-scatter.30.cloned.1.call-update) | async-done | bytes 1048592 | tf_op jit(solution)/shard_map/reduce_scatter | solution.py:248
  1538.8 181.0 %reduce-scatter.32.cloned.1.call-done = f32[128,2048]{1,0:T(8,128)} async-done(((f32[2048,2048]{1,0:T(8,128)}), f32[128,2048]{1,0:T(8,128)}) %reduce-scatter.32.cloned.1.call-update) | async-done | bytes 1048592 | tf_op jit(solution)/shard_map/reduce_scatter | solution.py:249
  1719.8 181.1 %reduce-scatter.28.cloned.1.call-done = f32[128,2048]{1,0:T(8,128)} async-done(((f32[2048,2048]{1,0:T(8,128)}), f32[128,2048]{1,0:T(8,128)}) %reduce-scatter.28.cloned.1.call-update) | async-done | bytes 1048592 | tf_op jit(solution)/shard_map/reduce_scatter | solution.py:328
  1901.0 181.0 %reduce-scatter.26.cloned.1.call-done = f32[128,2048]{1,0:T(8,128)} async-done(((f32[2048,2048]{1,0:T(8,128)}), f32[128,2048]{1,0:T(8,128)}) %reduce-scatter.26.cloned.1.call-update) | async-done | bytes 1048592 | tf_op jit(solution)/shard_map/reduce_scatter | solution.py:327
  2081.9 107.2 %reduce-scatter.22.cloned.1.call-done = f32[128,1024]{1,0:T(8,128)} async-done(((f32[2048,1024]{1,0:T(8,128)}), f32[128,1024]{1,0:T(8,128)}) %reduce-scatter.22.cloned.1.call-update) | async-done | bytes 524304 | tf_op jit(solution)/shard_map/reduce_scatter | solution.py:325
  2189.2 107.8 %reduce-scatter.20.cloned.1.call-done = f32[128,1024]{1,0:T(8,128)} async-done(((f32[2048,1024]{1,0:T(8,128)}), f32[128,1024]{1,0:T(8,128)}) %reduce-scatter.20.cloned.1.call-update) | async-done | bytes 524304 | tf_op jit(solution)/shard_map/reduce_scatter | solution.py:324
  2296.9 181.7 %reduce-scatter.24.cloned.1.call-done = f32[128,2048]{1,0:T(8,128)} async-done(((f32[2048,2048]{1,0:T(8,128)}), f32[128,2048]{1,0:T(8,128)}) %reduce-scatter.24.cloned.1.call-update) | async-done | bytes 1048592 | tf_op jit(solution)/shard_map/reduce_scatter | solution.py:326
  (281 shorter events, 121.5 us)
Async XLA Ops:
  7.2 48.6 %copy-start.63 = (s32[16]{0:T(128)S(1)}, s32[16]{0:T(128)}, u32[]{:S(2)}) copy-start(s32[16]{0:T(128)} %param.19) | copy-start | bytes 196
  7.2 51.2 %copy-start.64 = (s32[2]{0:T(128)S(1)}, s32[2]{0:T(128)}, u32[]{:S(2)}) copy-start(s32[2]{0:T(128)} %param.20) | copy-start | bytes 28
  7.2 65.6 %all-gather.16.cloned.1.call-start = ((), (), s32[]{:S(2)}) async-start(), calls=%async_computation.11 | async-start | bytes 1572864 | tf_op jit(solution)/shard_map/all_gather | solution.py:85
  8.4 42.3 %copy-start.50 = (f32[128]{0:T(128)}, f32[128]{0:T(128)S(1)}, u32[]{:S(2)}) copy-start(f32[128]{0:T(128)S(1)} %broadcast_multiply_fusion.10) | copy-start | bytes 1540
  9.8 41.0 %copy-start.55 = (f32[128]{0:T(128)}, f32[128]{0:T(128)S(1)}, u32[]{:S(2)}) copy-start(f32[128]{0:T(128)S(1)} %add_rsqrt_fusion.2) | copy-start | bytes 1540
  33.1 17.7 copy-start.38
  53.1 72.4 %all-gather.24.cloned.1.call-start = ((), (), s32[]{:S(2)}) async-start(), calls=%async_computation.15 | async-start | bytes 4456448 | tf_op jit(solution)/shard_map/all_gather | solution.py:123
  53.8 122.7 %all-gather.22.cloned.1.call-start = ((), (), s32[]{:S(2)}) async-start(), calls=%async_computation.14 | async-start | bytes 4456448 | tf_op jit(solution)/shard_map/all_gather | solution.py:122
  54.5 196.9 %all-gather.20.cloned.1.call-start = ((), (), s32[]{:S(2)}) async-start(), calls=%async_computation.13 | async-start | bytes 8912896 | tf_op jit(solution)/shard_map/all_gather | solution.py:124
  55.1 271.2 %all-gather.18.cloned.1.call-start = ((), (), s32[]{:S(2)}) async-start(), calls=%async_computation.12 | async-start | bytes 8912896 | tf_op jit(solution)/shard_map/all_gather | solution.py:125
  55.7 384.0 %all-reduce.9.cloned.1.call-start = ((), (), s32[]{:S(2)}) async-start(), calls=%async_computation.16 | async-start | bytes 8388608 | tf_op jit(solution)/shard_map/psum | solution.py:204
  61.6 378.1 %copy-start.48 = (f32[2]{0:T(128)}, f32[2]{0:T(128)S(1)}, u32[]{:S(2)}) copy-start(f32[2]{0:T(128)S(1)} %compare_convert_fusion) | copy-start | bytes 28
  62.3 201.7 %copy-start.61 = (f32[4]{0:T(128)}, f32[4]{0:T(128)S(1)}, u32[]{:S(2)}) copy-start(f32[4]{0:T(128)S(1)} %subtract_log_fusion) | copy-start | bytes 52
  62.4 194.7 %copy-start.41 = (f32[256,4]{0,1:T(4,128)}, f32[256,4]{0,1:T(4,128)S(1)}, u32[]{:S(2)}) copy-start(f32[256,4]{0,1:T(4,128)S(1)} %get-tuple-element.64) | copy-start | bytes 12292
  62.4 380.3 %copy-start.43 = (f32[256,4]{0,1:T(4,128)}, f32[256,4]{0,1:T(4,128)S(1)}, u32[]{:S(2)}) copy-start(f32[256,4]{0,1:T(4,128)S(1)} %get-tuple-element.65) | copy-start | bytes 12292
  129.2 47.4 %copy-start = (bf16[256,2048]{1,0:T(8,128)(2,1)S(1)}, bf16[256,2048]{1,0:T(8,128)(2,1)}, u32[]{:S(2)}) copy-start(bf16[256,2048]{1,0:T(8,128)(2,1)} %all-gather.16.cloned.1.call-done) | copy-start | bytes 3145732
  185.0 79.1 %copy-start.23 = (bf16[256,4,128]{2,0,1:T(8,128)(2,1)}, bf16[256,4,128]{2,0,1:T(8,128)(2,1)S(1)}, u32[]{:S(2)}) copy-start(bf16[256,4,128]{2,0,1:T(8,128)(2,1)S(1)} %get-tuple-element.51) | copy-start | bytes 786436
  257.1 80.0 %copy-start.5 = (bf16[256,2048]{1,0:T(8,128)(2,1)}, bf16[256,2048]{1,0:T(8,128)(2,1)S(1)}, u32[]{:S(2)}) copy-start(bf16[256,2048]{1,0:T(8,128)(2,1)S(1)} %convolution_convert_fusion) | copy-start | bytes 3145732
  261.1 254.1 %all-gather.26.cloned.1.call-start = ((), (), s32[]{:S(2)}) async-start(), calls=%async_computation.17 | async-start | bytes 8912896 | tf_op jit(solution)/shard_map/all_gather | solution.py:126
  261.9 298.4 %reduce-scatter.12.cloned.1.call-start = ((), (), s32[]{:S(2)}) async-start(), calls=%async_computation.18 | async-start | bytes 3145728 | tf_op jit(solution)/shard_map/reduce_scatter | solution.py:89
  264.1 178.6 %copy-start.12 = (bf16[256,4,256]{2,0,1:T(8,128)(2,1)}, bf16[256,4,256]{2,0,1:T(8,128)(2,1)S(1)}, u32[]{:S(2)}) copy-start(bf16[256,4,256]{2,0,1:T(8,128)(2,1)S(1)} %fusion.41) | copy-start | bytes 1572868
  445.8 76.6 %copy-start.16 = (bf16[256,4,512]{0,2,1:T(8,128)(2,1)}, bf16[256,4,512]{0,2,1:T(8,128)(2,1)S(1)}, u32[]{:S(2)}) copy-start(bf16[256,4,512]{0,2,1:T(8,128)(2,1)S(1)} %multiply_convert_fusion.3) | copy-start | bytes 3145732
  522.4 19.8 copy-start.60
  522.4 107.2 %all-gather.30.cloned.1.call-start = ((), (), s32[]{:S(2)}) async-start(), calls=%async_computation.20 | async-start | bytes 8912896 | tf_op jit(solution)/shard_map/all_gather | solution.py:131
  523.1 128.3 %all-gather.28.cloned.1.call-start = ((), (), s32[]{:S(2)}) async-start(), calls=%async_computation.19 | async-start | bytes 1572864 | tf_op jit(solution)/shard_map/all_gather | solution.py:85
  563.7 164.2 %all-gather.32.cloned.1.call-start = ((), (), s32[]{:S(2)}) async-start(), calls=%async_computation.21 | async-start | bytes 8912896 | tf_op jit(solution)/shard_map/all_gather | solution.py:132
  564.4 201.6 %reduce-scatter.14.cloned.1.call-start = ((), (), s32[]{:S(2)}) async-start(), calls=%async_computation.22 | async-start | bytes 3145728 | tf_op jit(solution)/shard_map/reduce_scatter | solution.py:89
  735.4 98.8 %all-gather.34.cloned.1.call-start = ((), (), s32[]{:S(2)}) async-start(), calls=%async_computation.23 | async-start | bytes 1572864 | tf_op jit(solution)/shard_map/all_gather | solution.py:85
  811.8 70.2 %reduce-scatter.16.cloned.1.call-start = ((), (), s32[]{:S(2)}) async-start(), calls=%async_computation.24 | async-start | bytes 3145728 | tf_op jit(solution)/shard_map/reduce_scatter | solution.py:89
  850.0 59.0 %all-gather.36.cloned.1.call-start = ((), (), s32[]{:S(2)}) async-start(), calls=%async_computation.25 | async-start | bytes 1572864 | tf_op jit(solution)/shard_map/all_gather | solution.py:85
  887.6 505.4 %reduce-scatter.18.cloned.1.call-start = ((), (), s32[]{:S(2)}) async-start(), calls=%async_computation.26 | async-start | bytes 3145728 | tf_op jit(solution)/shard_map/reduce_scatter | solution.py:89
  909.0 7.2 copy-start.3
  921.9 7.2 collective-permute-start
  930.0 92.7 %collective-permute-start.1 = (f32[2,4,256,512]{3,2,1,0:T(8,128)S(1)}, f32[2,4,256,512]{3,2,1,0:T(8,128)S(1)}, u32[]{:S(2)}, u32[]{:S(2)}) collective-permute-start(f32[2,4,256,512]{3,2,1,0:T(8,128)S(1)} %fusion.56), channel_id=1, source_target_pairs={{0,4},{2,6},{4,0},{6,2},{8,12},{10,14},{12,8},{14,10},{16,20},{18,... | collective-permute-start | bytes 12582920 | tf_op jit(solution)/shard_map/ppermute | solution.py:284
  1024.0 91.8 %collective-permute-start.2 = (f32[2,4,256,512]{3,2,1,0:T(8,128)S(1)}, f32[2,4,256,512]{3,2,1,0:T(8,128)S(1)}, u32[]{:S(2)}, u32[]{:S(2)}) collective-permute-start(f32[2,4,256,512]{3,2,1,0:T(8,128)S(1)} %fusion.140), channel_id=1, source_target_pairs={{0,8},{2,10},{4,12},{6,14},{8,0},{10,2},{12,4},{14,6},{16,24},{18,... | collective-permute-start | bytes 12582920 | tf_op jit(solution)/shard_map/ppermute | solution.py:284
  1118.8 182.0 %collective-permute-start.3 = (f32[2,4,256,512]{3,2,1,0:T(8,128)}, f32[2,4,256,512]{3,2,1,0:T(8,128)}, u32[]{:S(2)}, u32[]{:S(2)}) collective-permute-start(f32[2,4,256,512]{3,2,1,0:T(8,128)} %add.239), channel_id=1, source_target_pairs={{0,16},{2,18},{4,20},{6,22},{8,24},{10,26},{12,28},{14,30},{16,0},... | collective-permute-start | bytes 12582920 | tf_op jit(solution)/shard_map/ppermute | solution.py:284
  1131.5 174.3 %copy-start.42 = (f32[256,4]{0,1:T(4,128)S(1)}, f32[256,4]{0,1:T(4,128)}, u32[]{:S(2)}) copy-start(f32[256,4]{0,1:T(4,128)} %copy-done.41) | copy-start | bytes 12292
  1313.0 7.3 slice-start
  1314.3 6.0 slice-start.1
  1324.2 214.6 %reduce-scatter.30.cloned.1.call-start = ((), (), s32[]{:S(2)}) async-start(), calls=%async_computation.32 | async-start | bytes 17825792 | tf_op jit(solution)/shard_map/reduce_scatter | solution.py:248
  1335.3 384.5 %reduce-scatter.32.cloned.1.call-start = ((), (), s32[]{:S(2)}) async-start(), calls=%async_computation.33 | async-start | bytes 17825792 | tf_op jit(solution)/shard_map/reduce_scatter | solution.py:249
  1345.9 555.0 %reduce-scatter.28.cloned.1.call-start = ((), (), s32[]{:S(2)}) async-start(), calls=%async_computation.31 | async-start | bytes 17825792 | tf_op jit(solution)/shard_map/reduce_scatter | solution.py:328
  1356.5 725.4 %reduce-scatter.26.cloned.1.call-start = ((), (), s32[]{:S(2)}) async-start(), calls=%async_computation.30 | async-start | bytes 17825792 | tf_op jit(solution)/shard_map/reduce_scatter | solution.py:327
  1366.1 823.1 %reduce-scatter.22.cloned.1.call-start = ((), (), s32[]{:S(2)}) async-start(), calls=%async_computation.28 | async-start | bytes 8912896 | tf_op jit(solution)/shard_map/reduce_scatter | solution.py:325
  1372.3 924.7 %reduce-scatter.20.cloned.1.call-start = ((), (), s32[]{:S(2)}) async-start(), calls=%async_computation.27 | async-start | bytes 8912896 | tf_op jit(solution)/shard_map/reduce_scatter | solution.py:324
  1378.2 1100.5 %reduce-scatter.24.cloned.1.call-start = ((), (), s32[]{:S(2)}) async-start(), calls=%async_computation.29 | async-start | bytes 17825792 | tf_op jit(solution)/shard_map/reduce_scatter | solution.py:326
  1389.8 76.7 %copy-start.20 = (f32[128,2048]{1,0:T(8,128)S(1)}, f32[128,2048]{1,0:T(8,128)}, u32[]{:S(2)}) copy-start(f32[128,2048]{1,0:T(8,128)} %get-tuple-element.36) | copy-start | bytes 3145732
  1393.0 73.4 %copy-start.18 = (f32[128,2048]{1,0:T(8,128)S(1)}, f32[128,2048]{1,0:T(8,128)}, u32[]{:S(2)}) copy-start(f32[128,2048]{1,0:T(8,128)} %reduce-scatter.18.cloned.1.call-done) | copy-start | bytes 3145732
  (47 other events, 90.8 us)
Sparse Core Ops, SparseCore 0:
  53.2 19.6 all-gather.15
  75.0 50.3 all-gather.23
  127.6 48.8 all-gather.21
  178.5 72.8 all-gather.19
  253.4 72.8 all-gather.17
  329.9 109.7 all-reduce.8
  441.8 73.4 all-gather.25
  522.5 30.4 reduce-scatter.11
  555.2 74.3 all-gather.29
  631.5 19.8 all-gather.27
  653.6 74.2 all-gather.31
  735.5 30.4 reduce-scatter.13
  811.9 22.1 all-gather.33
  850.1 31.8 reduce-scatter.15
  887.7 21.2 all-gather.35
  1324.3 31.8 reduce-scatter.17
  1360.8 177.9 reduce-scatter.29
  1543.4 176.4 reduce-scatter.31
  1724.5 176.4 reduce-scatter.27
  1905.5 176.4 reduce-scatter.25
  2086.6 102.5 reduce-scatter.21
  2193.8 103.0 reduce-scatter.19
  2301.6 176.9 reduce-scatter.23
